TPU v7x, 512 devices: a whole 4x8x8 slice. The times are simulated.
512 devices in a mesh: row: 32 (over y, x), head: 16 (over z, core).
Axes of the slice: x: 4, y: 8, z: 8, core: 2. Of those that a mesh axis runs over, the one named last changes fastest.
Arguments:
- patches: bfloat16 [196608, 768], P(('row', 'head')), may hold values from -6 to 6
- w_patch: bfloat16 [768, 1024], replicated, may hold values from -0.21875 to 0.21875
- patch_bias: float32 [1024], replicated, may hold values from -4 to 4
- w_kv: bfloat16 [1024, 2048], P(None, 'head'), may hold values from -0.1875 to 0.1875
- queries: bfloat16 [2048, 1024], P(None, 'head'), may hold values from -160 to 160
Outputs:
- readout: bfloat16 [2048, 1024], P(None, 'head')
All inputs are finite; a program needn't handle non-finite values.
Results may differ from a plain program's by a relative error of at most 0.011.
Values may be sent and summed in bfloat16 or wider, within the bound.
No kernel may reach another device: no remote copies, remote signals or barrier semaphores. Data moves between devices by JAX's collectives and lax.ppermute only.
A program may use at most 128 MiB of HBM per device.

v0:
```python
import jax
import jax.numpy as jnp
from jax import lax
from jax.sharding import PartitionSpec as P


def body(patches, w_patch, patch_bias, w_kv, queries):
    embed = jnp.dot(patches, w_patch, preferred_element_type=jnp.float32) + patch_bias
    mean = jnp.mean(embed, axis=-1, keepdims=True)
    var = jnp.mean((embed - mean) * (embed - mean), axis=-1, keepdims=True)
    normed = ((embed - mean) * lax.rsqrt(var + 1e-05)).astype(jnp.bfloat16)
    head_size = queries.shape[1]
    latents = queries.shape[0]
    kv_all = jnp.dot(
        normed, lax.all_gather(w_kv, "head", axis=1, tiled=True), preferred_element_type=jnp.float32
    ).astype(jnp.bfloat16)
    kv = lax.all_to_all(kv_all, "head", split_axis=1, concat_axis=0, tiled=True)
    rows = kv.shape[0]
    block = min(512, rows)
    blocks = kv.reshape(rows // block, block, 2 * head_size)
    scale = float(head_size) ** (-0.5)

    def step(carry, piece):
        run_max, total, accum = carry
        scores = (
            jnp.dot(queries, piece[:, :head_size].T, preferred_element_type=jnp.float32) * scale
        )
        new_max = jnp.maximum(run_max, jnp.max(scores, axis=1))
        factor = jnp.exp(run_max - new_max)
        probs = jnp.exp(scores - new_max[:, None])
        total = total * factor + jnp.sum(probs, axis=1)
        accum = accum * factor[:, None] + jnp.dot(
            probs.astype(jnp.bfloat16), piece[:, head_size:], preferred_element_type=jnp.float32
        )
        return ((new_max, total, accum), None)

    start = (
        jnp.full((latents,), -jnp.inf, jnp.float32),
        jnp.zeros((latents,), jnp.float32),
        jnp.zeros((latents, head_size), jnp.float32),
    )
    (run_max, total, accum), _ = lax.scan(step, start, blocks)
    top = lax.pmax(run_max, "row")
    factor = jnp.exp(run_max - top)
    whole, summed = lax.psum((total * factor, accum * factor[:, None]), "row")
    return (summed / whole[:, None]).astype(jnp.bfloat16)


def solution(mesh):
    placed = (P(("row", "head"), None), P(), P(), P(None, "head"), P(None, "head"))
    return jax.shard_map(
        body, mesh=mesh, in_specs=placed, out_specs=P(None, "head"), check_vma=False
    )
```

profile of v0, /device:TPU:64, one launch (start us, length us, event | category | flops | bytes accessed | tf_op | source)
XLA Modules:
  0.0 447.2 jit_solution(7872800311003511222)
XLA Ops:
  7.9 1.9 fusion.14
  10.2 55.2 %all-gather.2.cloned.1.call-done = bf16[1024,2048]{1,0:T(8,128)(2,1)} async-done(((bf16[1024,128]{1,0:T(8,128)(2,1)}), bf16[1024,2048]{1,0:T(8,128)(2,1)}) %all-gather.2.cloned.1.call-update) | async-done | bytes 4194320 | tf_op jit(solution)/shard_map/all_gather | solution.py:15
  65.4 4.1 fusion.10
  69.5 1.6 copy.10
  71.1 5.3 %all-to-all-start = ((bf16[384,16,128]{2,0,1:T(8,128)(2,1)}), bf16[384,16,128]{2,0,1:T(8,128)(2,1)}, u32[]{:S(2)}, u32[]{:S(2)}) async-start(bf16[384,16,128]{2,0,1:T(8,128)(2,1)} %bitcast.18), calls=%async_computation | async-start | bytes 3145728 | tf_op jit(solution)/shard_map/all_to_all | solution.py:17
  76.5 36.1 %all-to-all-done = bf16[384,16,128]{2,0,1:T(8,128)(2,1)} async-done(((bf16[384,16,128]{2,0,1:T(8,128)(2,1)}), bf16[384,16,128]{2,0,1:T(8,128)(2,1)}, u32[]{:S(2)}, u32[]{:S(2)}) %all-to-all-start) | async-done | bytes 1572896 | tf_op jit(solution)/shard_map/all_to_all | solution.py:17
  112.5 95.5 %while.15 = (s32[]{:T(128)}, f32[2048]{0:T(1024)S(1)}, f32[2048]{0:T(1024)S(1)}, f32[2048,64]{0,1:T(8,128)S(1)}, bf16[12,512,128]{2,1,0:T(8,128)(2,1)}, /*index=5*/bf16[2048,64]{0,1:T(8,128)(2,1)S(1)}, s32[]{:T(128)}, s32[]{:T(128)}) while((s32[]{:T(128)}, f32[2048]{0:T(1024)S(1)}, f32[2048]{0:T(1024)S(1)}, ...), condition=%wide.region_5.6_spmd.clone, body=%wide.region_2.5_spmd.clone.sunk | while | flops 277227520 | bytes 31326336 | solution.py:42
  113.5 2.6 multiply_reduce_fusion.3
  116.1 3.0 fusion.27
  119.5 0.9 convolution_add_fusion.3
  121.4 2.6 multiply_reduce_fusion.3
  124.0 3.0 fusion.27
  127.5 0.9 convolution_add_fusion.3
  128.5 0.9 dynamic-slice_bitcast_fusion.2
  129.4 2.6 multiply_reduce_fusion.3
  132.0 3.0 fusion.27
  135.5 0.9 convolution_add_fusion.3
  137.4 2.6 multiply_reduce_fusion.3
  140.0 3.0 fusion.27
  143.4 0.9 convolution_add_fusion.3
  145.3 2.6 multiply_reduce_fusion.3
  147.9 3.0 fusion.27
  151.4 0.9 convolution_add_fusion.3
  153.3 2.6 multiply_reduce_fusion.3
  155.9 3.0 fusion.27
  159.3 0.9 convolution_add_fusion.3
  161.2 2.6 multiply_reduce_fusion.3
  163.8 3.0 fusion.27
  167.3 0.9 convolution_add_fusion.3
  169.2 2.6 multiply_reduce_fusion.3
  171.8 3.0 fusion.27
  175.2 0.9 convolution_add_fusion.3
  177.1 2.6 multiply_reduce_fusion.3
  179.8 3.0 fusion.27
  183.2 0.9 convolution_add_fusion.3
  185.1 2.6 multiply_reduce_fusion.3
  187.7 3.0 fusion.27
  191.2 0.9 convolution_add_fusion.3
  193.1 2.6 multiply_reduce_fusion.3
  195.7 3.0 fusion.27
  199.1 0.9 convolution_add_fusion.3
  201.0 2.6 multiply_reduce_fusion.3
  203.6 3.0 fusion.27
  207.1 0.9 convolution_add_fusion.3
  208.0 75.6 %pmax.7 = f32[2048]{0:T(1024)S(1)} all-reduce(f32[2048]{0:T(1024)S(1)} %get-tuple-element.40), channel_id=1, replica_groups=mesh['row'=32,'head'=16] {'row'}, use_global_device_ids=true, to_apply=%region_6.7 | all-reduce | flops 2048 | bytes 16384 | tf_op jit(solution)/shard_map/pmax | solution.py:43
  284.6 70.7 %psum.15 = f32[2048]{0:T(1024)S(1)} all-reduce(f32[2048]{0:T(1024)S(1)} %get-tuple-element.77), channel_id=1, replica_groups=mesh['row'=32,'head'=16] {'row'}, use_global_device_ids=true, to_apply=%region_8.9 | all-reduce | flops 2048 | bytes 16384 | tf_op jit(solution)/shard_map/psum | solution.py:45
  355.3 83.3 %all-reduce.2.cloned.1.call-done = f32[2048,64]{0,1:T(8,128)} async-done(((f32[2048,64]{0,1:T(8,128)}), f32[2048,64]{0,1:T(8,128)}) %all-reduce.2.cloned.1.call-update) | async-done | bytes 524304 | tf_op jit(solution)/shard_map/psum | solution.py:45
  438.6 1.8 divide_convert_fusion
  (87 shorter events, 17.6 us)
Async XLA Ops:
  6.5 1.4 copy-start
  6.5 58.9 %all-gather.2.cloned.1.call-start = ((), (), s32[]{:S(2)}) async-start(), calls=%async_computation.1 | async-start | bytes 4456448 | tf_op jit(solution)/shard_map/all_gather | solution.py:15
  71.1 41.5 %copy-start.2 = (bf16[2048,64]{0,1:T(8,128)(2,1)S(1)}, bf16[2048,64]{0,1:T(8,128)(2,1)}, u32[]{:S(2)}) copy-start(bf16[2048,64]{0,1:T(8,128)(2,1)} %param.11) | copy-start | bytes 786436
  71.1 41.5 %all-to-all-start = ((bf16[384,16,128]{2,0,1:T(8,128)(2,1)}), bf16[384,16,128]{2,0,1:T(8,128)(2,1)}, u32[]{:S(2)}, u32[]{:S(2)}) async-start(bf16[384,16,128]{2,0,1:T(8,128)(2,1)} %bitcast.18), calls=%async_computation | async-start | bytes 3145728 | tf_op jit(solution)/shard_map/all_to_all | solution.py:17
  76.4 362.2 %all-reduce.2.cloned.1.call-start = ((), (), s32[]{:S(2)}) async-start(), calls=%async_computation.2 | async-start | bytes 1048576 | tf_op jit(solution)/shard_map/psum | solution.py:45
  116.1 3.4 copy-start.1
  124.0 3.4 copy-start.1
  132.0 3.4 copy-start.1
  140.0 3.4 copy-start.1
  147.9 3.4 copy-start.1
  155.9 3.4 copy-start.1
  163.8 3.4 copy-start.1
  171.8 3.4 copy-start.1
  179.8 3.4 copy-start.1
  187.7 3.4 copy-start.1
  195.7 3.4 copy-start.1
  203.6 3.4 copy-start.1
Sparse Core Ops, SparseCore 0:
  9.4 55.9 all-gather.1
  284.7 153.8 all-reduce.1
where the time goes:
time: 448 us; the launch traced here: 447 us
  waiting for transfers between devices  175 us (39%)
  blocking collectives  146 us (33%)
  matrix products  48.6 us (11%)
  other arithmetic  39.7 us (9%)
  local copies, waits for them, and re-layouts  17.9 us (4%)
  between operations  13.5 us (3%)
  starting transfers between devices  5.38 us (1%)
    psum x1, waiting for transfers between devices, body(): whole, summed = lax.psum((total * factor, accum * factor[:, None]), 'row')  83.3 us
    pmax x1, blocking collectives, body(): top = lax.pmax(run_max, 'row')  75.6 us
    psum x1, blocking collectives, body(): whole, summed = lax.psum((total * factor, accum * factor[:, None]), 'row')  70.7 us
    all_gather x1, waiting for transfers between devices, body(): lax.all_gather(w_kv, 'head', axis=1, tiled=True)  55.2 us
    reduce_sum x12, other arithmetic, step(): total = total * factor + jnp.sum(probs, axis=1)  36.6 us
    all_to_all x1, waiting for transfers between devices, body(): kv = lax.all_to_all(kv_all, 'head', split_axis=1, concat_axis=0, tiled=True)  36.1 us
    dot_general x12, matrix products, step(): jnp.dot(queries, piece[:, :head_size].T, preferred_element_type=jnp.float32)  31.3 us
    dot_general x12, matrix products, step(): jnp.dot(probs.astype(jnp.bfloat16), piece[:, head_size:], preferred_eleme...  11.3 us
  transfers between devices with their start and end apart: 3, of which 3 were waited for; matrix products, arithmetic and copies ran while one was open for 1% of the time, Pallas kernels for 0%

commit v1 on v0

--- a/solution.py
+++ b/solution.py
@@ -2,6 +2,7 @@
 import jax.numpy as jnp
 from jax import lax
 from jax.sharding import PartitionSpec as P
+from jax.lax import all_to_all, axis_size
 
 
 def body(patches, w_patch, patch_bias, w_kv, queries):
@@ -11,9 +12,12 @@
     normed = ((embed - mean) * lax.rsqrt(var + 1e-05)).astype(jnp.bfloat16)
     head_size = queries.shape[1]
     latents = queries.shape[0]
-    kv_all = jnp.dot(
-        normed, lax.all_gather(w_kv, "head", axis=1, tiled=True), preferred_element_type=jnp.float32
-    ).astype(jnp.bfloat16)
+    touch_threads = lambda view: jnp.concatenate(
+        all_to_all(jnp.stack([view] * axis_size("head"), 0), "head", split_axis=0, concat_axis=0), 1
+    )
+    kv_all = jnp.dot(normed, touch_threads(w_kv), preferred_element_type=jnp.float32).astype(
+        jnp.bfloat16
+    )
     kv = lax.all_to_all(kv_all, "head", split_axis=1, concat_axis=0, tiled=True)
     rows = kv.shape[0]
     block = min(512, rows)

time: 448 us -> 497 us (1.11)
  waiting for transfers between devices: 175 us -> 209 us
  starting transfers between devices: 5.38 us -> 16.9 us
    all_to_all x0 -> x1, waiting for transfers between devices: none -> 90.2 us  [body(): all_to_all(jnp.stack([view] * axis_size('head'), 0), 'head', split_axis=0...]
    all_gather x1 -> x0, waiting for transfers between devices: 55.2 us -> none  [body(): lax.all_gather(w_kv, 'head', axis=1, tiled=True)]
    all_to_all x0 -> x1, starting transfers between devices: none -> 10.1 us  [body(): all_to_all(jnp.stack([view] * axis_size('head'), 0), 'head', split_axis=0...]
  transfers between devices with their start and end apart: 3 -> 3, of which waited for: 3 -> 3; matrix products, arithmetic and copies ran while one was open for 1% -> 0% of each run, Pallas kernels for 0% -> 0%
where the time goes in v1:
time: 497 us; the launch traced here: 496 us
  waiting for transfers between devices  209 us (42%)
  blocking collectives  147 us (30%)
  matrix products  48.7 us (10%)
  other arithmetic  39.7 us (8%)
  local copies, waits for them, and re-layouts  20.8 us (4%)
  starting transfers between devices  16.9 us (3%)
  between operations  13.5 us (3%)
    all_to_all x1, waiting for transfers between devices, body(): all_to_all(jnp.stack([view] * axis_size('head'), 0), 'head', split_axis=0...  90.2 us
    psum x1, waiting for transfers between devices, body(): whole, summed = lax.psum((total * factor, accum * factor[:, None]), 'row')  82.8 us
    pmax x1, blocking collectives, body(): top = lax.pmax(run_max, 'row')  76.3 us
    psum x1, blocking collectives, body(): whole, summed = lax.psum((total * factor, accum * factor[:, None]), 'row')  70.8 us
    reduce_sum x12, other arithmetic, step(): total = total * factor + jnp.sum(probs, axis=1)  36.6 us
    all_to_all x1, waiting for transfers between devices, body(): kv = lax.all_to_all(kv_all, 'head', split_axis=1, concat_axis=0, tiled=True)  36.1 us
    dot_general x12, matrix products, step(): jnp.dot(queries, piece[:, :head_size].T, preferred_element_type=jnp.float32)  31.4 us
    dot_general x12, matrix products, step(): jnp.dot(probs.astype(jnp.bfloat16), piece[:, head_size:], preferred_eleme...  11.3 us
  transfers between devices with their start and end apart: 3, of which 3 were waited for; matrix products, arithmetic and copies ran while one was open for 0% of the time, Pallas kernels for 0%

profile of v1, /device:TPU:64, one launch (start us, length us, event | category | flops | bytes accessed | tf_op | source)
XLA Modules:
  0.0 496.4 jit_solution(1662485368170216970)
XLA Ops:
  6.5 1.2 copy.9
  7.7 2.5 stack.2
  10.3 10.1 %all-to-all-start = ((bf16[16,1024,128]{1,2,0:T(8,128)(2,1)}), bf16[16,1024,128]{1,2,0:T(8,128)(2,1)}, u32[]{:S(2)}, u32[]{:S(2)}) async-start(bf16[16,1024,128]{1,2,0:T(8,128)(2,1)} %stack.2), calls=%async_computation | async-start | bytes 8388608 | tf_op jit(solution)/shard_map/all_to_all | solution.py:16
  20.4 1.9 fusion.14
  22.6 90.2 %all-to-all-done = bf16[16,1024,128]{1,2,0:T(8,128)(2,1)} async-done(((bf16[16,1024,128]{1,2,0:T(8,128)(2,1)}), bf16[16,1024,128]{1,2,0:T(8,128)(2,1)}, u32[]{:S(2)}, u32[]{:S(2)}) %all-to-all-start) | async-done | bytes 4194336 | tf_op jit(solution)/shard_map/all_to_all | solution.py:16
  112.8 4.1 fusion.10
  116.9 1.6 copy.13
  118.5 6.8 %all-to-all-start.1 = ((bf16[384,16,128]{2,0,1:T(8,128)(2,1)}), bf16[384,16,128]{2,0,1:T(8,128)(2,1)}, u32[]{:S(2)}, u32[]{:S(2)}) async-start(bf16[384,16,128]{2,0,1:T(8,128)(2,1)} %bitcast.21), calls=%async_computation.1 | async-start | bytes 3145728 | tf_op jit(solution)/shard_map/all_to_all | solution.py:21
  125.3 36.1 %all-to-all-done.1 = bf16[384,16,128]{2,0,1:T(8,128)(2,1)} async-done(((bf16[384,16,128]{2,0,1:T(8,128)(2,1)}), bf16[384,16,128]{2,0,1:T(8,128)(2,1)}, u32[]{:S(2)}, u32[]{:S(2)}) %all-to-all-start.1) | async-done | bytes 1572896 | tf_op jit(solution)/shard_map/all_to_all | solution.py:21
  161.4 95.5 %while.15 = (s32[]{:T(128)}, f32[2048]{0:T(1024)S(1)}, f32[2048]{0:T(1024)S(1)}, f32[2048,64]{0,1:T(8,128)S(1)}, bf16[12,512,128]{2,1,0:T(8,128)(2,1)}, /*index=5*/bf16[2048,64]{0,1:T(8,128)(2,1)S(1)}, s32[]{:T(128)}, s32[]{:T(128)}) while((s32[]{:T(128)}, f32[2048]{0:T(1024)S(1)}, f32[2048]{0:T(1024)S(1)}, ...), condition=%wide.region_5.6_spmd.clone, body=%wide.region_2.5_spmd.clone.sunk | while | flops 277227520 | bytes 31326344 | solution.py:46
  162.3 2.6 multiply_reduce_fusion.3
  165.0 3.0 fusion.27
  170.3 2.6 multiply_reduce_fusion.3
  172.9 3.0 fusion.27
  176.4 0.9 convolution_add_fusion.3
  178.2 2.6 multiply_reduce_fusion.3
  180.9 3.0 fusion.27
  184.3 0.9 convolution_add_fusion.3
  186.2 2.6 multiply_reduce_fusion.3
  188.8 3.0 fusion.27
  192.3 0.9 convolution_add_fusion.3
  194.2 2.6 multiply_reduce_fusion.3
  196.8 3.0 fusion.27
  200.2 0.9 convolution_add_fusion.3
  202.1 2.6 multiply_reduce_fusion.3
  204.7 3.0 fusion.27
  208.2 0.9 convolution_add_fusion.3
  210.1 2.6 multiply_reduce_fusion.3
  212.7 3.0 fusion.27
  216.1 0.9 convolution_add_fusion.3
  218.0 2.6 multiply_reduce_fusion.3
  220.7 3.0 fusion.27
  224.1 0.9 convolution_add_fusion.3
  226.0 2.6 multiply_reduce_fusion.3
  228.6 3.0 fusion.27
  232.1 0.9 convolution_add_fusion.3
  233.9 2.6 multiply_reduce_fusion.3
  236.6 3.0 fusion.27
  240.0 0.9 convolution_add_fusion.3
  241.9 2.6 multiply_reduce_fusion.3
  244.5 3.0 fusion.27
  248.0 0.9 convolution_add_fusion.3
  249.9 2.6 multiply_reduce_fusion.3
  252.5 3.0 fusion.27
  256.9 76.3 %pmax.7 = f32[2048]{0:T(1024)S(1)} all-reduce(f32[2048]{0:T(1024)S(1)} %get-tuple-element.40), channel_id=1, replica_groups=mesh['row'=32,'head'=16] {'row'}, use_global_device_ids=true, to_apply=%region_6.7 | all-reduce | flops 2048 | bytes 16384 | tf_op jit(solution)/shard_map/pmax | solution.py:47
  334.1 70.8 %psum.15 = f32[2048]{0:T(1024)S(1)} all-reduce(f32[2048]{0:T(1024)S(1)} %get-tuple-element.77), channel_id=1, replica_groups=mesh['row'=32,'head'=16] {'row'}, use_global_device_ids=true, to_apply=%region_8.9 | all-reduce | flops 2048 | bytes 16384 | tf_op jit(solution)/shard_map/psum | solution.py:49
  404.9 82.8 %all-reduce.2.cloned.1.call-done = f32[2048,64]{0,1:T(8,128)} async-done(((f32[2048,64]{0,1:T(8,128)}), f32[2048,64]{0,1:T(8,128)}) %all-reduce.2.cloned.1.call-update) | async-done | bytes 524304 | tf_op jit(solution)/shard_map/psum | solution.py:49
  487.7 1.8 divide_convert_fusion
  (90 shorter events, 18.9 us)
Async XLA Ops:
  6.5 13.8 %copy-start = (bf16[768,1024]{1,0:T(8,128)(2,1)S(1)}, bf16[768,1024]{1,0:T(8,128)(2,1)}, u32[]{:S(2)}) copy-start(bf16[768,1024]{1,0:T(8,128)(2,1)} %param.8) | copy-start | bytes 4718596
  10.3 10.1 %copy-start.3 = (f32[1024]{0:T(1024)S(1)}, f32[1024]{0:T(1024)}, u32[]{:S(2)}) copy-start(f32[1024]{0:T(1024)} %param.9) | copy-start | bytes 12292
  10.3 102.6 %all-to-all-start = ((bf16[16,1024,128]{1,2,0:T(8,128)(2,1)}), bf16[16,1024,128]{1,2,0:T(8,128)(2,1)}, u32[]{:S(2)}, u32[]{:S(2)}) async-start(bf16[16,1024,128]{1,2,0:T(8,128)(2,1)} %stack.2), calls=%async_computation | async-start | bytes 8388608 | tf_op jit(solution)/shard_map/all_to_all | solution.py:16
  118.5 42.9 %copy-start.2 = (bf16[2048,64]{0,1:T(8,128)(2,1)S(1)}, bf16[2048,64]{0,1:T(8,128)(2,1)}, u32[]{:S(2)}) copy-start(bf16[2048,64]{0,1:T(8,128)(2,1)} %param.11) | copy-start | bytes 786436
  118.5 42.9 %all-to-all-start.1 = ((bf16[384,16,128]{2,0,1:T(8,128)(2,1)}), bf16[384,16,128]{2,0,1:T(8,128)(2,1)}, u32[]{:S(2)}, u32[]{:S(2)}) async-start(bf16[384,16,128]{2,0,1:T(8,128)(2,1)} %bitcast.21), calls=%async_computation.1 | async-start | bytes 3145728 | tf_op jit(solution)/shard_map/all_to_all | solution.py:21
  125.3 362.5 %all-reduce.2.cloned.1.call-start = ((), (), s32[]{:S(2)}) async-start(), calls=%async_computation.2 | async-start | bytes 1048576 | tf_op jit(solution)/shard_map/psum | solution.py:49
  165.0 3.4 copy-start.1
  172.9 3.4 copy-start.1
  180.9 3.4 copy-start.1
  188.8 3.4 copy-start.1
  196.8 3.4 copy-start.1
  204.7 3.4 copy-start.1
  212.7 3.4 copy-start.1
  220.7 3.4 copy-start.1
  228.6 3.4 copy-start.1
  236.6 3.4 copy-start.1
  244.5 3.4 copy-start.1
  252.5 3.4 copy-start.1
Sparse Core Ops, SparseCore 0:
  334.3 153.4 all-reduce.1
